TPU v7x, 512 devices: a whole 4x8x8 slice. The times are simulated.
512 devices in a mesh: stream: 128 (over y, z, core), vert: 4 (over x).
Axes of the slice: x: 4, y: 8, z: 8, core: 2. Of those that a mesh axis runs over, the one named last changes fastest.
Arguments:
- particles: float32 [4096, 4, 7, 128], P('stream', 'vert'), may hold values from -4 to 4, as said below
- phase_flags: int32 [4096, 4, 128], P('stream', 'vert'), may hold values 0 or 1
- neighbours: int32 [4096, 4, 4], P('stream', 'vert'), may hold values from 0 to 7, as said below
- history: bfloat16 [4096, 4, 3, 126, 128], P('stream', 'vert'), may hold values from -160 to 160
- basis_start: float32 [128, 64], replicated, may hold values from -0.5 to 0.5
Outputs:
- new_state: float32 [4096, 4, 7, 128], P('stream', 'vert')
- filtered: float32 [4096, 4, 3, 128], P('stream', 'vert')
Inputs may be any that keep to these rules, and one draw needn't show every extreme that they name: `particles`: rows 0 to 2 of a particle lie in 0 to 2, rows 3 to 5 in -4 to 4, row 6 in 0.97 to 1.03. `neighbours`: the 4 codes of one block are distinct.
All inputs are finite; a program needn't handle non-finite values. No bound on the sum of `phase_flags` on one device may be relied on, other than what follows from the above.
Results may differ from a plain program's by a relative error of at most 0.0003.
Values sent between devices are 32-bit elements; how exact they have to be, the bound alone decides.
A program may use at most 64 MiB of HBM per device.

v0:
```python
import math
import jax
import jax.numpy as jnp
from jax import lax
from jax.sharding import PartitionSpec as P

POD_ITERS = 4
ALPHA_KERNEL = 21.0 / (16.0 * math.pi)
VOLUME = 1.0 / 16.0
STIFFNESS = 100.0 / 7.0
TIME_STEP = 0.02
GRAVITY = 1.0
SEDIMENT_EXTRA = 1.65


def with_halo(block, sides, width):
    for axis, dim in sides:
        count = lax.axis_size(axis)
        forward = [(i, i + 1) for i in range(count - 1)]
        backward = [(target, source) for source, target in forward]
        low = lax.ppermute(
            lax.slice_in_dim(block, block.shape[dim] - width, None, axis=dim), axis, forward
        )
        high = lax.ppermute(lax.slice_in_dim(block, 0, width, axis=dim), axis, backward)
        block = jnp.concatenate([low, block, high], axis=dim)
    return block


def forces(own_block, near_blocks, cell_shifts):
    separation = (
        own_block[:, None, 0:3, :, None]
        - near_blocks[:, :, 0:3, None, :]
        - cell_shifts[:, :, :, None, None]
    )
    radius = jnp.sqrt(jnp.sum(separation * separation, axis=2))
    kernel_reach = jnp.maximum(1.0 - 0.5 * radius, 0.0)
    kernel_slope = -5.0 * ALPHA_KERNEL * kernel_reach**3 * near_blocks[:, :, 6, None, :]
    closing = own_block[:, None, 3:6, :, None] - near_blocks[:, :, 3:6, None, :]
    density_rate = jnp.sum(kernel_slope * jnp.sum(closing * separation, axis=2), axis=(1, 3))
    pressure_term = kernel_slope * (own_block[:, None, 7, :, None] + near_blocks[:, :, 7, None, :])
    acceleration = -jnp.sum(pressure_term[:, :, None] * separation, axis=(1, 4))
    return (acceleration, density_rate)


def block_layout(neighbours):
    blocks_stream, blocks_vert = (neighbours.shape[0], neighbours.shape[1])
    offset_code = neighbours + (neighbours >= 4).astype(jnp.int32)
    zero_codes = jnp.zeros((blocks_stream, blocks_vert, 1), jnp.int32)
    stream_step = jnp.concatenate([zero_codes, offset_code // 3 - 1], axis=-1)
    vert_step = jnp.concatenate([zero_codes, offset_code % 3 - 1], axis=-1)
    stream_place = jnp.arange(blocks_stream, dtype=jnp.int32)[:, None, None]
    vert_place = jnp.arange(blocks_vert, dtype=jnp.int32)[None, :, None]
    near_index = (stream_place + 1 + stream_step) * (blocks_vert + 2) + (vert_place + 1 + vert_step)
    list_width = near_index.shape[2]
    cell_shifts = jnp.stack(
        [
            2.0 * stream_step.astype(jnp.float32),
            jnp.zeros(stream_step.shape, jnp.float32),
            2.0 * vert_step.astype(jnp.float32),
        ],
        axis=-1,
    )
    return (near_index.reshape(-1, list_width), cell_shifts.reshape(-1, list_width, 3))


def make_payload(particles, rest_density, particle_mass):
    relative = particles[:, :, 6]
    pressure = STIFFNESS * (relative**7 - 1.0) / (rest_density * relative * relative)
    return jnp.concatenate(
        [particles[:, :, 0:6], particle_mass[:, :, None], pressure[:, :, None]], axis=2
    )


def interact(payload, extended, near_index, cell_shifts, group_limit):
    block_count = payload.shape[0] * payload.shape[1]
    group_size = math.gcd(block_count, group_limit)
    flat_blocks = extended.reshape(-1, 8, payload.shape[3])
    list_width = near_index.shape[1]

    def one_group(pieces):
        own_block, index_part, shift_part = pieces
        near_blocks = jnp.take(flat_blocks, index_part, axis=0)
        return forces(own_block, near_blocks, shift_part)

    acceleration, density_rate = lax.map(
        one_group,
        (
            payload.reshape(block_count // group_size, group_size, 8, -1),
            near_index.reshape(-1, group_size, list_width),
            cell_shifts.reshape(-1, group_size, list_width, 3),
        ),
    )
    return (
        acceleration.reshape(payload.shape[0], payload.shape[1], 3, -1),
        density_rate.reshape(payload.shape[0], payload.shape[1], -1),
    )


def update(particles, rest_density, acceleration, density_rate):
    gravity_vector = jnp.array([0.0, 0.0, -GRAVITY], jnp.float32)[:, None]
    velocity = particles[:, :, 3:6] + TIME_STEP * (acceleration + gravity_vector)
    position = particles[:, :, 0:3] + TIME_STEP * velocity
    relative = particles[:, :, 6] + TIME_STEP * density_rate / rest_density
    return jnp.concatenate([position, velocity, relative[:, :, None]], axis=2)


def orthonormal(matrix):
    for repeat in range(2):
        inner_product = jnp.dot(matrix.T, matrix, precision=lax.Precision.HIGHEST)
        factor = jnp.linalg.cholesky(inner_product)
        matrix = lax.linalg.triangular_solve(
            factor, matrix, left_side=False, lower=True, transpose_a=True
        )
    return matrix


def pod_weights(gram_matrix, basis_start):
    basis_now = orthonormal(basis_start)
    for iteration in range(POD_ITERS):
        basis_now = orthonormal(jnp.dot(gram_matrix, basis_now, precision=lax.Precision.HIGHEST))
    return jnp.dot(basis_now, basis_now[-1], precision=lax.Precision.HIGHEST)


def extend(payload):
    return with_halo(payload, (("stream", 0), ("vert", 1)), 1)


def advance(particles, rest_density, particle_mass, near_index, cell_shifts):
    payload = make_payload(particles, rest_density, particle_mass)
    extended = extend(payload)
    acceleration, density_rate = interact(payload, extended, near_index, cell_shifts, 4)
    return update(particles, rest_density, acceleration, density_rate)


def body(particles, phase_flags, neighbours, history, basis_start):
    rest_density = 1.0 + SEDIMENT_EXTRA * phase_flags.astype(jnp.float32)
    particle_mass = rest_density * VOLUME
    near_index, cell_shifts = block_layout(neighbours)
    first_state = advance(particles, rest_density, particle_mass, near_index, cell_shifts)
    second_state = advance(first_state, rest_density, particle_mass, near_index, cell_shifts)
    new_snapshots = jnp.stack([first_state[:, :, 3:6], second_state[:, :, 3:6]], axis=3).astype(
        jnp.bfloat16
    )
    snapshots = jnp.concatenate([history, new_snapshots], axis=3)
    gram_matrix = lax.psum(
        jnp.einsum("abcsp,abctp->st", snapshots, snapshots, preferred_element_type=jnp.float32),
        ("stream", "vert"),
    )
    weights = pod_weights(gram_matrix, basis_start)
    filtered = jnp.einsum(
        "abcsp,s->abcp", snapshots.astype(jnp.float32), weights, precision=lax.Precision.HIGHEST
    )
    return (second_state, filtered)


def solution(mesh):
    in_specs = (
        P("stream", "vert", None, None),
        P("stream", "vert", None),
        P("stream", "vert", None),
        P("stream", "vert", None, None, None),
        P(),
    )
    out_specs = (P("stream", "vert", None, None), P("stream", "vert", None, None))
    return jax.shard_map(body, mesh=mesh, in_specs=in_specs, out_specs=out_specs, check_vma=False)
```

profile of v0, /device:TPU:1, one launch (start us, length us, event | category | flops | bytes accessed | tf_op | source)
XLA Modules:
  0.0 584.5 jit_solution(12489457789824271340)
XLA Ops:
  9.6 5.4 collective-permute-start
  15.0 4.7 collective-permute-start.1
  21.8 5.8 %cholesky.164 = f32[64,64]{1,0:T(8,128)S(1)} custom-call(f32[64,64]{1,0:T(8,128)S(1)} %fusion.36), custom_call_target="Cholesky" | custom-call | tf_op jit(solution)/shard_map/jit(cholesky)/cholesky | solution.py:110
  29.0 4.9 custom-call.14
  34.4 5.8 %cholesky.175 = f32[64,64]{1,0:T(8,128)S(1)} custom-call(f32[64,64]{1,0:T(8,128)S(1)} %fusion.34), custom_call_target="Cholesky" | custom-call | tf_op jit(solution)/shard_map/jit(cholesky)/cholesky | solution.py:110
  45.3 4.2 collective-permute-done.3
  50.5 48.7 %while.24 = (s32[]{:T(128)}, f32[8,4,3,128]{3,2,1,0:T(4,128)S(1)}, f32[8,4,128]{2,1,0:T(4,128)S(1)}, f32[8,4,8,128]{3,1,0,2:T(4,128)S(1)}, s32[8,4,5]{2,1,0:T(4,...) while((s32[]{:T(128)}, f32[8,4,3,128]{3,2,1,0:T(4,128)S(1)}, ...), condition=%wide.region_5.7_spmd, body=%wide.region_0.6_spmd.sunk | while | flops 15424634 | bytes 10094649 | solution.py:85
  100.0 3.7 collective-permute-start.4
  103.7 1.9 collective-permute-start.5
  106.3 4.9 custom-call.15
  111.3 3.1 collective-permute-start.6
  116.7 3.1 copy.166
  123.3 74.8 %while.25 = (s32[]{:T(128)}, f32[8,4,3,128]{3,2,1,0:T(4,128)}, f32[8,4,128]{2,1,0:T(4,128)}, f32[8,4,8,128]{3,1,2,0:T(4,128)}, s32[8,4,5]{2,1,0:T(4,128)}, /*ind...) while((s32[]{:T(128)}, f32[8,4,3,128]{3,2,1,0:T(4,128)}, f32[8,4,128]{2,1,0:T(4,128)}, ...), condition=%wide.region_11.13_spmd, body=%wide.region_6.12_spmd.sunk | while | flops 15424634 | bytes 10093617 | solution.py:85
  128.9 1.8 multiply_reduce_fusion.18
  199.1 2.5 fusion.6
  202.5 268.8 %all-reduce.4.cloned.1.call-done = f32[128,128]{1,0:T(8,128)} async-done(((f32[128,128]{1,0:T(8,128)}), f32[128,128]{1,0:T(8,128)}) %all-reduce.4.cloned.1.call-update) | async-done | bytes 65552 | tf_op jit(solution)/shard_map/psum | solution.py:145
  472.7 5.8 %cholesky.186 = f32[64,64]{1,0:T(8,128)S(1)} custom-call(f32[64,64]{1,0:T(8,128)S(1)} %fusion.32), custom_call_target="Cholesky" | custom-call | tf_op jit(solution)/shard_map/jit(cholesky)/cholesky | solution.py:110
  479.9 4.9 custom-call.16
  485.4 5.8 %cholesky.197 = f32[64,64]{1,0:T(8,128)S(1)} custom-call(f32[64,64]{1,0:T(8,128)S(1)} %fusion.30), custom_call_target="Cholesky" | custom-call | tf_op jit(solution)/shard_map/jit(cholesky)/cholesky | solution.py:110
  492.6 4.9 custom-call.17
  499.1 5.8 %cholesky.208 = f32[64,64]{1,0:T(8,128)S(1)} custom-call(f32[64,64]{1,0:T(8,128)S(1)} %fusion.28), custom_call_target="Cholesky" | custom-call | tf_op jit(solution)/shard_map/jit(cholesky)/cholesky | solution.py:110
  506.3 4.9 custom-call.18
  511.7 5.8 %cholesky.219 = f32[64,64]{1,0:T(8,128)S(1)} custom-call(f32[64,64]{1,0:T(8,128)S(1)} %fusion.26), custom_call_target="Cholesky" | custom-call | tf_op jit(solution)/shard_map/jit(cholesky)/cholesky | solution.py:110
  518.9 4.9 custom-call.19
  524.6 5.8 %cholesky.230 = f32[64,64]{1,0:T(8,128)S(1)} custom-call(f32[64,64]{1,0:T(8,128)S(1)} %fusion.24), custom_call_target="Cholesky" | custom-call | tf_op jit(solution)/shard_map/jit(cholesky)/cholesky | solution.py:110
  531.8 4.9 custom-call.20
  537.2 6.0 %cholesky.241 = f32[64,64]{1,0:T(8,128)S(1)} custom-call(f32[64,64]{1,0:T(8,128)S(1)} %fusion.22), custom_call_target="Cholesky" | custom-call | tf_op jit(solution)/shard_map/jit(cholesky)/cholesky | solution.py:110
  544.6 4.9 custom-call.21
  550.3 5.8 %cholesky.252 = f32[64,64]{1,0:T(8,128)S(1)} custom-call(f32[64,64]{1,0:T(8,128)S(1)} %fusion.20), custom_call_target="Cholesky" | custom-call | tf_op jit(solution)/shard_map/jit(cholesky)/cholesky | solution.py:110
  557.4 4.9 custom-call.22
  562.9 5.8 %cholesky.263 = f32[64,64]{1,0:T(8,128)S(1)} custom-call(f32[64,64]{1,0:T(8,128)S(1)} %fusion.18), custom_call_target="Cholesky" | custom-call | tf_op jit(solution)/shard_map/jit(cholesky)/cholesky | solution.py:110
  570.1 4.9 custom-call.23
  (553 shorter events, 160.8 us)
Async XLA Ops:
  7.2 14.3 %copy-start = (f32[128,64]{0,1:T(8,128)S(1)}, f32[128,64]{0,1:T(8,128)}, u32[]{:S(2)}) copy-start(f32[128,64]{0,1:T(8,128)} %param.20) | copy-start | bytes 98308
  7.2 464.1 %all-reduce.4.cloned.1.call-start = ((), (), s32[]{:S(2)}) async-start(), calls=%async_computation | async-start | bytes 131072 | tf_op jit(solution)/shard_map/psum | solution.py:145
  9.6 30.8 %collective-permute-start = (f32[1,1,8,128]{3,0,2,1:T(1,128)S(1)}, f32[1,1,8,128]{3,0,2,1:T(1,128)S(1)}, u32[]{:S(2)}, u32[]{:S(2)}) collective-permute-start(f32[1,1,8,128]{3,0,2,1:T(1,128)S(1)} %get-tuple-element.168), channel_id=1, source_target_pairs={{0,4},{4,8},{8,12},{12,16},{16,20},{20,24},{24,28},{28,32},{32,36}... | collective-permute-start | bytes 12296 | tf_op jit(solution)/shard_map/ppermute | solution.py:21
  15.0 25.4 %collective-permute-start.1 = (f32[1,1,8,128]{3,0,2,1:T(1,128)S(1)}, f32[1,1,8,128]{3,0,2,1:T(1,128)S(1)}, u32[]{:S(2)}, u32[]{:S(2)}) collective-permute-start(f32[1,1,8,128]{3,0,2,1:T(1,128)S(1)} %get-tuple-element.169), channel_id=1, source_target_pairs={{4,0},{8,4},{12,8},{16,12},{20,16},{24,20},{28,24},{32,28},{36,32}... | collective-permute-start | bytes 12296 | tf_op jit(solution)/shard_map/ppermute | solution.py:24
  40.5 4.9 collective-permute-start.2
  41.8 7.8 %collective-permute-start.3 = (f32[34,1,8,128]{3,0,2,1:T(8,128)S(1)}, f32[34,1,8,128]{3,0,2,1:T(8,128)S(1)}, u32[]{:S(2)}, u32[]{:S(2)}) collective-permute-start(f32[34,1,8,128]{3,0,2,1:T(8,128)S(1)} %pad_maximum_fusion.2), channel_id=1, source_target_pairs={{1,0},{2,1},{3,2},{5,4},{6,5},{7,6},{9,8},{10,9},{11,10},{13,12},{... | collective-permute-start | bytes 417800 | tf_op jit(solution)/shard_map/ppermute | solution.py:24
  50.5 48.8 %copy-start.3 = (s32[32,1,128]{2,1,0:T(1,128)S(1)}, s32[32,1,128]{2,1,0:T(1,128)}, u32[]{:S(2)}) copy-start(s32[32,1,128]{2,1,0:T(1,128)} %param.17) | copy-start | bytes 49156
  50.5 49.4 %copy-start.10 = (f32[3]{0:T(128)S(1)}, f32[3]{0:T(128)}, u32[]{:S(2)}) copy-start(f32[3]{0:T(128)} %constant.134.clone) | copy-start | bytes 40
  99.2 0.6 copy-start.2
  99.2 16.7 %copy-start.7 = (s32[8,4,5]{2,1,0:T(4,128)}, s32[8,4,5]{2,1,0:T(4,128)S(1)}, u32[]{:S(2)}) copy-start(s32[8,4,5]{2,1,0:T(4,128)S(1)} %get-tuple-element.364) | copy-start | bytes 1924
  99.2 0.6 copy-start.4
  100.0 11.2 %collective-permute-start.4 = (f32[1,1,8,128]{3,2,1,0:T(8,128)S(1)}, f32[1,1,8,128]{3,2,1,0:T(8,128)S(1)}, u32[]{:S(2)}, u32[]{:S(2)}) collective-permute-start(f32[1,1,8,128]{3,2,1,0:T(8,128)S(1)} %get-tuple-element.166), channel_id=1, source_target_pairs={{0,4},{4,8},{8,12},{12,16},{16,20},{20,24},{24,28},{28,32},{32,36}... | collective-permute-start | bytes 12296 | tf_op jit(solution)/shard_map/ppermute | solution.py:21
  103.7 7.5 %collective-permute-start.5 = (f32[1,1,8,128]{3,2,1,0:T(8,128)S(1)}, f32[1,1,8,128]{3,2,1,0:T(8,128)S(1)}, u32[]{:S(2)}, u32[]{:S(2)}) collective-permute-start(f32[1,1,8,128]{3,2,1,0:T(8,128)S(1)} %get-tuple-element.167), channel_id=1, source_target_pairs={{4,0},{8,4},{12,8},{16,12},{20,16},{24,20},{28,24},{32,28},{36,32}... | collective-permute-start | bytes 12296 | tf_op jit(solution)/shard_map/ppermute | solution.py:24
  111.3 9.9 %collective-permute-start.6 = (f32[34,1,8,128]{3,2,1,0:T(8,128)S(1)}, f32[34,1,8,128]{3,2,1,0:T(8,128)S(1)}, u32[]{:S(2)}, u32[]{:S(2)}) collective-permute-start(f32[34,1,8,128]{3,2,1,0:T(8,128)S(1)} %pad_maximum_fusion.3), channel_id=1, source_target_pairs={{0,1},{1,2},{2,3},{4,5},{5,6},{6,7},{8,9},{9,10},{10,11},{12,13},{... | collective-permute-start | bytes 417800 | tf_op jit(solution)/shard_map/ppermute | solution.py:21
  114.4 6.8 %collective-permute-start.7 = (f32[34,1,8,128]{3,2,1,0:T(8,128)S(1)}, f32[34,1,8,128]{3,2,1,0:T(8,128)S(1)}, u32[]{:S(2)}, u32[]{:S(2)}) collective-permute-start(f32[34,1,8,128]{3,2,1,0:T(8,128)S(1)} %pad_maximum_fusion.3), channel_id=1, source_target_pairs={{1,0},{2,1},{3,2},{5,4},{6,5},{7,6},{9,8},{10,9},{11,10},{13,12},{... | collective-permute-start | bytes 417800 | tf_op jit(solution)/shard_map/ppermute | solution.py:24
  199.0 2.6 copy-start.8
  199.0 2.6 copy-start.5
  199.1 272.2 %copy-start.6 = (f32[128,64]{0,1:T(8,128)S(1)}, f32[128,64]{0,1:T(8,128)}, u32[]{:S(2)}) copy-start(f32[128,64]{0,1:T(8,128)} %convolution_bitcast_fusion.8) | copy-start | bytes 98308
  471.3 52.8 %copy-start.1 = (f32[128,128]{1,0:T(8,128)S(1)}, f32[128,128]{1,0:T(8,128)}, u32[]{:S(2)}) copy-start(f32[128,128]{1,0:T(8,128)} %all-reduce.4.cloned.1.call-done) | copy-start | bytes 196612
  511.4 64.1 %copy-start.9 = (bf16[32,1,3,1,128]{4,3,2,0,1:T(2,128)(2,1)S(1)}, bf16[32,1,3,1,128]{4,3,2,0,1:T(2,128)(2,1)}, u32[]{:S(2)}) copy-start(bf16[32,1,3,1,128]{4,3,2,0,1:T(2,128)(2,1)} %copy.167) | copy-start | bytes 73732
Sparse Core Ops, SparseCore 0:
  201.7 269.5 all-reduce.3
where the time goes:
time: 587 us; the launch traced here: 584 us
  waiting for transfers between devices  275 us (47%)
  other arithmetic  200 us (34%)
  local copies, waits for them, and re-layouts  58.8 us (10%)
  starting transfers between devices  22.9 us (4%)
  between operations  14.9 us (3%)
  matrix products  11.6 us (2%)
    psum x1, waiting for transfers between devices, body(): lax.psum(jnp.einsum('abcsp,abctp->st', snapshots, snapshots, preferred_el...  269 us
    another operation x30, other arithmetic, orthonormal(): factor = jnp.linalg.cholesky(inner_product)  65.3 us
    another operation x20, other arithmetic, orthonormal(): lax.linalg.triangular_solve(factor, matrix, left_side=False, lower=True,...  55.5 us
    reduce_sum x16, other arithmetic, forces(): jnp.sum(closing * separation, axis=2)  28.4 us
    gather x16, local copies, waits for them, and re-layouts, one_group(): near_blocks = jnp.take(flat_blocks, index_part, axis=0)  25 us
    ppermute x4, starting transfers between devices, with_halo(): lax.ppermute(lax.slice_in_dim(block, block.shape[dim] - width, None, axis...  13.5 us
    reduce_sum x16, other arithmetic, forces(): radius = jnp.sqrt(jnp.sum(separation * separation, axis=2))  11.9 us
  transfers between devices with their start and end apart: 9, of which 3 were waited for; matrix products, arithmetic and copies ran while one was open for 6% of the time, Pallas kernels for 0%

commit v1 on v0

--- a/solution.py
+++ b/solution.py
@@ -143,8 +143,11 @@
     )
     snapshots = jnp.concatenate([history, new_snapshots], axis=3)
     gram_matrix = lax.psum(
-        jnp.einsum("abcsp,abctp->st", snapshots, snapshots, preferred_element_type=jnp.float32),
-        ("stream", "vert"),
+        lax.psum(
+            jnp.einsum("abcsp,abctp->st", snapshots, snapshots, preferred_element_type=jnp.float32),
+            "vert",
+        ),
+        "stream",
     )
     weights = pod_weights(gram_matrix, basis_start)
     filtered = jnp.einsum(

time: 587 us -> 561 us (0.956)
  waiting for transfers between devices: 275 us -> 249 us
  local copies, waits for them, and re-layouts: 58.8 us -> 50.2 us
  other arithmetic: 200 us -> 207 us
    psum x1, waiting for transfers between devices: 269 us -> 55.7 us  [body(): lax.psum(jnp.einsum('abcsp,abctp->st', snapshots, snapshots, preferred_el...]
    psum x0 -> x1, waiting for transfers between devices: none -> 188 us  [body(): lax.psum(lax.psum(jnp.einsum('abcsp,abctp->st', snapshots, snapshots, pre...]
    gather x16, local copies, waits for them, and re-layouts: 25 us -> 17.1 us  [one_group(): near_blocks = jnp.take(flat_blocks, index_part, axis=0)]
  transfers between devices with their start and end apart: 9 -> 10, of which waited for: 3 -> 4; matrix products, arithmetic and copies ran while one was open for 6% -> 6% of each run, Pallas kernels for 0% -> 0%
where the time goes in v1:
time: 561 us; the launch traced here: 558 us
  waiting for transfers between devices  249 us (44%)
  other arithmetic  207 us (37%)
  local copies, waits for them, and re-layouts  50.2 us (9%)
  starting transfers between devices  23.1 us (4%)
  between operations  14.9 us (3%)
  matrix products  11.6 us (2%)
    psum x1, waiting for transfers between devices, body(): lax.psum(lax.psum(jnp.einsum('abcsp,abctp->st', snapshots, snapshots, pre...  188 us
    another operation x30, other arithmetic, orthonormal(): factor = jnp.linalg.cholesky(inner_product)  65.6 us
    psum x1, waiting for transfers between devices, body(): lax.psum(jnp.einsum('abcsp,abctp->st', snapshots, snapshots, preferred_el...  55.7 us
    another operation x20, other arithmetic, orthonormal(): lax.linalg.triangular_solve(factor, matrix, left_side=False, lower=True,...  55.7 us
    reduce_sum x16, other arithmetic, forces(): jnp.sum(closing * separation, axis=2)  29.2 us
    gather x16, local copies, waits for them, and re-layouts, one_group(): near_blocks = jnp.take(flat_blocks, index_part, axis=0)  17.1 us
    ppermute x4, starting transfers between devices, with_halo(): lax.ppermute(lax.slice_in_dim(block, block.shape[dim] - width, None, axis...  13.5 us
    reduce_sum x16, other arithmetic, forces(): radius = jnp.sqrt(jnp.sum(separation * separation, axis=2))  12.1 us
  transfers between devices with their start and end apart: 10, of which 4 were waited for; matrix products, arithmetic and copies ran while one was open for 6% of the time, Pallas kernels for 0%

profile of v1, /device:TPU:1, one launch (start us, length us, event | category | flops | bytes accessed | tf_op | source)
XLA Modules:
  0.0 558.4 jit_solution(14935533596909725406)
XLA Ops:
  9.6 5.4 collective-permute-start
  15.0 4.7 collective-permute-start.1
  21.8 5.8 %cholesky.164 = f32[64,64]{1,0:T(8,128)S(1)} custom-call(f32[64,64]{1,0:T(8,128)S(1)} %fusion.36), custom_call_target="Cholesky" | custom-call | tf_op jit(solution)/shard_map/jit(cholesky)/cholesky | solution.py:110
  29.0 4.9 custom-call.14
  34.4 5.8 %cholesky.175 = f32[64,64]{1,0:T(8,128)S(1)} custom-call(f32[64,64]{1,0:T(8,128)S(1)} %fusion.34), custom_call_target="Cholesky" | custom-call | tf_op jit(solution)/shard_map/jit(cholesky)/cholesky | solution.py:110
  45.4 4.2 collective-permute-done.3
  49.8 47.1 %while.24 = (s32[]{:T(128)}, f32[8,4,3,128]{3,2,1,0:T(4,128)S(1)}, f32[8,4,128]{2,1,0:T(4,128)S(1)}, f32[8,4,8,128]{3,1,0,2:T(4,128)S(1)}, s32[8,4,5]{2,1,0:T(4,...) while((s32[]{:T(128)}, f32[8,4,3,128]{3,2,1,0:T(4,128)S(1)}, ...), condition=%wide.region_5.7_spmd, body=%wide.region_0.6_spmd.sunk | while | flops 15424634 | bytes 10094649 | solution.py:85
  97.7 3.7 collective-permute-start.4
  101.4 1.9 collective-permute-start.5
  104.0 4.9 custom-call.15
  109.0 3.1 collective-permute-start.6
  114.4 3.1 copy.166
  121.0 75.0 %while.25 = (s32[]{:T(128)}, f32[8,4,3,128]{3,2,1,0:T(4,128)}, f32[8,4,128]{2,1,0:T(4,128)}, f32[8,4,8,128]{3,1,2,0:T(4,128)}, s32[8,4,5]{2,1,0:T(4,128)}, /*ind...) while((s32[]{:T(128)}, f32[8,4,3,128]{3,2,1,0:T(4,128)}, f32[8,4,128]{2,1,0:T(4,128)}, ...), condition=%wide.region_11.13_spmd, body=%wide.region_6.12_spmd.sunk | while | flops 15424634 | bytes 10109033 | solution.py:85
  197.0 2.5 fusion.6
  199.9 55.7 %all-reduce.5.cloned.1.call-done = f32[128,128]{1,0:T(8,128)} async-done(((f32[128,128]{1,0:T(8,128)}), f32[128,128]{1,0:T(8,128)}) %all-reduce.5.cloned.1.call-update) | async-done | bytes 65552 | tf_op jit(solution)/shard_map/psum | solution.py:146
  256.4 188.5 %all-reduce.7.cloned.1.call-done = f32[128,128]{1,0:T(8,128)} async-done(((f32[128,128]{1,0:T(8,128)}), f32[128,128]{1,0:T(8,128)}) %all-reduce.7.cloned.1.call-update) | async-done | bytes 65552 | tf_op jit(solution)/shard_map/psum | solution.py:145
  446.3 5.8 %cholesky.186 = f32[64,64]{1,0:T(8,128)S(1)} custom-call(f32[64,64]{1,0:T(8,128)S(1)} %fusion.32), custom_call_target="Cholesky" | custom-call | tf_op jit(solution)/shard_map/jit(cholesky)/cholesky | solution.py:110
  453.5 4.9 custom-call.16
  458.9 5.8 %cholesky.197 = f32[64,64]{1,0:T(8,128)S(1)} custom-call(f32[64,64]{1,0:T(8,128)S(1)} %fusion.30), custom_call_target="Cholesky" | custom-call | tf_op jit(solution)/shard_map/jit(cholesky)/cholesky | solution.py:110
  466.1 4.9 custom-call.17
  472.6 5.8 %cholesky.208 = f32[64,64]{1,0:T(8,128)S(1)} custom-call(f32[64,64]{1,0:T(8,128)S(1)} %fusion.28), custom_call_target="Cholesky" | custom-call | tf_op jit(solution)/shard_map/jit(cholesky)/cholesky | solution.py:110
  479.8 4.9 custom-call.18
  485.2 5.8 %cholesky.219 = f32[64,64]{1,0:T(8,128)S(1)} custom-call(f32[64,64]{1,0:T(8,128)S(1)} %fusion.26), custom_call_target="Cholesky" | custom-call | tf_op jit(solution)/shard_map/jit(cholesky)/cholesky | solution.py:110
  492.4 4.9 custom-call.19
  498.1 5.8 %cholesky.230 = f32[64,64]{1,0:T(8,128)S(1)} custom-call(f32[64,64]{1,0:T(8,128)S(1)} %fusion.24), custom_call_target="Cholesky" | custom-call | tf_op jit(solution)/shard_map/jit(cholesky)/cholesky | solution.py:110
  505.4 4.9 custom-call.20
  510.9 5.8 %cholesky.241 = f32[64,64]{1,0:T(8,128)S(1)} custom-call(f32[64,64]{1,0:T(8,128)S(1)} %fusion.22), custom_call_target="Cholesky" | custom-call | tf_op jit(solution)/shard_map/jit(cholesky)/cholesky | solution.py:110
  518.2 5.0 custom-call.21
  524.0 5.8 %cholesky.252 = f32[64,64]{1,0:T(8,128)S(1)} custom-call(f32[64,64]{1,0:T(8,128)S(1)} %fusion.20), custom_call_target="Cholesky" | custom-call | tf_op jit(solution)/shard_map/jit(cholesky)/cholesky | solution.py:110
  531.3 4.9 custom-call.22
  536.8 5.8 %cholesky.263 = f32[64,64]{1,0:T(8,128)S(1)} custom-call(f32[64,64]{1,0:T(8,128)S(1)} %fusion.18), custom_call_target="Cholesky" | custom-call | tf_op jit(solution)/shard_map/jit(cholesky)/cholesky | solution.py:110
  544.1 4.9 custom-call.23
  (590 shorter events, 161.2 us)
Async XLA Ops:
  7.2 14.3 %copy-start = (f32[128,64]{0,1:T(8,128)S(1)}, f32[128,64]{0,1:T(8,128)}, u32[]{:S(2)}) copy-start(f32[128,64]{0,1:T(8,128)} %param.20) | copy-start | bytes 98308
  7.2 248.4 %all-reduce.5.cloned.1.call-start = ((), (), s32[]{:S(2)}) async-start(), calls=%async_computation | async-start | bytes 131072 | tf_op jit(solution)/shard_map/psum | solution.py:146
  9.6 30.8 %collective-permute-start = (f32[1,1,8,128]{3,0,2,1:T(1,128)S(1)}, f32[1,1,8,128]{3,0,2,1:T(1,128)S(1)}, u32[]{:S(2)}, u32[]{:S(2)}) collective-permute-start(f32[1,1,8,128]{3,0,2,1:T(1,128)S(1)} %get-tuple-element.168), channel_id=1, source_target_pairs={{0,4},{4,8},{8,12},{12,16},{16,20},{20,24},{24,28},{28,32},{32,36}... | collective-permute-start | bytes 12296 | tf_op jit(solution)/shard_map/ppermute | solution.py:21
  15.0 25.4 %collective-permute-start.1 = (f32[1,1,8,128]{3,0,2,1:T(1,128)S(1)}, f32[1,1,8,128]{3,0,2,1:T(1,128)S(1)}, u32[]{:S(2)}, u32[]{:S(2)}) collective-permute-start(f32[1,1,8,128]{3,0,2,1:T(1,128)S(1)} %get-tuple-element.169), channel_id=1, source_target_pairs={{4,0},{8,4},{12,8},{16,12},{20,16},{24,20},{28,24},{32,28},{36,32}... | collective-permute-start | bytes 12296 | tf_op jit(solution)/shard_map/ppermute | solution.py:24
  40.5 4.9 collective-permute-start.2
  41.8 7.8 %collective-permute-start.3 = (f32[34,1,8,128]{3,0,2,1:T(8,128)S(1)}, f32[34,1,8,128]{3,0,2,1:T(8,128)S(1)}, u32[]{:S(2)}, u32[]{:S(2)}) collective-permute-start(f32[34,1,8,128]{3,0,2,1:T(8,128)S(1)} %pad_maximum_fusion.2), channel_id=1, source_target_pairs={{1,0},{2,1},{3,2},{5,4},{6,5},{7,6},{9,8},{10,9},{11,10},{13,12},{... | collective-permute-start | bytes 417800 | tf_op jit(solution)/shard_map/ppermute | solution.py:24
  49.8 47.1 %copy-start.4 = (s32[32,1,128]{2,1,0:T(1,128)S(1)}, s32[32,1,128]{2,1,0:T(1,128)}, u32[]{:S(2)}) copy-start(s32[32,1,128]{2,1,0:T(1,128)} %param.17) | copy-start | bytes 49156
  49.8 47.2 %copy-start.13 = (f32[3]{0:T(128)S(1)}, f32[3]{0:T(128)}, u32[]{:S(2)}) copy-start(f32[3]{0:T(128)} %constant.134.clone) | copy-start | bytes 40
  96.9 20.7 %copy-start.5 = (f32[8,4,128]{2,1,0:T(4,128)}, f32[8,4,128]{2,1,0:T(4,128)S(1)}, u32[]{:S(2)}) copy-start(f32[8,4,128]{2,1,0:T(4,128)S(1)} %broadcast_multiply_fusion.1) | copy-start | bytes 49156
  97.7 11.2 %collective-permute-start.4 = (f32[1,1,8,128]{3,2,1,0:T(8,128)S(1)}, f32[1,1,8,128]{3,2,1,0:T(8,128)S(1)}, u32[]{:S(2)}, u32[]{:S(2)}) collective-permute-start(f32[1,1,8,128]{3,2,1,0:T(8,128)S(1)} %get-tuple-element.166), channel_id=1, source_target_pairs={{0,4},{4,8},{8,12},{12,16},{16,20},{20,24},{24,28},{28,32},{32,36}... | collective-permute-start | bytes 12296 | tf_op jit(solution)/shard_map/ppermute | solution.py:21
  101.4 7.5 %collective-permute-start.5 = (f32[1,1,8,128]{3,2,1,0:T(8,128)S(1)}, f32[1,1,8,128]{3,2,1,0:T(8,128)S(1)}, u32[]{:S(2)}, u32[]{:S(2)}) collective-permute-start(f32[1,1,8,128]{3,2,1,0:T(8,128)S(1)} %get-tuple-element.167), channel_id=1, source_target_pairs={{4,0},{8,4},{12,8},{16,12},{20,16},{24,20},{28,24},{32,28},{36,32}... | collective-permute-start | bytes 12296 | tf_op jit(solution)/shard_map/ppermute | solution.py:24
  109.0 9.9 %collective-permute-start.6 = (f32[34,1,8,128]{3,2,1,0:T(8,128)S(1)}, f32[34,1,8,128]{3,2,1,0:T(8,128)S(1)}, u32[]{:S(2)}, u32[]{:S(2)}) collective-permute-start(f32[34,1,8,128]{3,2,1,0:T(8,128)S(1)} %pad_maximum_fusion.3), channel_id=1, source_target_pairs={{0,1},{1,2},{2,3},{4,5},{5,6},{6,7},{8,9},{9,10},{10,11},{12,13},{... | collective-permute-start | bytes 417800 | tf_op jit(solution)/shard_map/ppermute | solution.py:21
  112.1 6.8 %collective-permute-start.7 = (f32[34,1,8,128]{3,2,1,0:T(8,128)S(1)}, f32[34,1,8,128]{3,2,1,0:T(8,128)S(1)}, u32[]{:S(2)}, u32[]{:S(2)}) collective-permute-start(f32[34,1,8,128]{3,2,1,0:T(8,128)S(1)} %pad_maximum_fusion.3), channel_id=1, source_target_pairs={{1,0},{2,1},{3,2},{5,4},{6,5},{7,6},{9,8},{10,9},{11,10},{13,12},{... | collective-permute-start | bytes 417800 | tf_op jit(solution)/shard_map/ppermute | solution.py:24
  114.4 3.1 copy-start.8
  121.0 2.3 copy-start.2
  130.3 2.3 copy-start.2
  137.8 1.9 copy-start.3
  139.7 2.3 copy-start.2
  149.1 2.3 copy-start.2
  158.4 2.4 copy-start.2
  165.9 1.9 copy-start.3
  167.8 2.3 copy-start.2
  177.2 2.4 copy-start.2
  186.6 2.3 copy-start.2
  197.0 2.5 copy-start.11
  197.0 2.8 copy-start.9
  197.0 2.9 copy-start.6
  197.0 247.9 %copy-start.7 = (f32[128,64]{0,1:T(8,128)S(1)}, f32[128,64]{0,1:T(8,128)}, u32[]{:S(2)}) copy-start(f32[128,64]{0,1:T(8,128)} %convolution_bitcast_fusion.8) | copy-start | bytes 98308
  199.5 245.3 %all-reduce.7.cloned.1.call-start = ((), (), s32[]{:S(2)}) async-start(), calls=%async_computation.1 | async-start | bytes 131072 | tf_op jit(solution)/shard_map/psum | solution.py:145
  444.8 52.7 %copy-start.1 = (f32[128,128]{1,0:T(8,128)S(1)}, f32[128,128]{1,0:T(8,128)}, u32[]{:S(2)}) copy-start(f32[128,128]{1,0:T(8,128)} %all-reduce.7.cloned.1.call-done) | copy-start | bytes 196612
  484.9 64.6 %copy-start.10 = (bf16[32,1,3,1,128]{4,3,2,0,1:T(2,128)(2,1)S(1)}, bf16[32,1,3,1,128]{4,3,2,0,1:T(2,128)(2,1)}, u32[]{:S(2)}) copy-start(bf16[32,1,3,1,128]{4,3,2,0,1:T(2,128)(2,1)} %copy.167) | copy-start | bytes 73732
  485.0 64.6 %copy-start.12 = (bf16[32,1,3,1,128]{4,3,2,0,1:T(2,128)(2,1)S(1)}, bf16[32,1,3,1,128]{4,3,2,0,1:T(2,128)(2,1)}, u32[]{:S(2)}) copy-start(bf16[32,1,3,1,128]{4,3,2,0,1:T(2,128)(2,1)} %copy-done.11) | copy-start | bytes 73732
  (6 other events, 11.5 us)
Sparse Core Ops, SparseCore 0:
  199.6 55.8 all-reduce.4
  258.8 186.0 all-reduce.6
